TPU v7x, 256 devices: a whole 4x4x8 slice. The times are simulated.
256 devices in a mesh: blk: 32 (over x_lo, z, core), head: 8 (over y, x_hi).
Axes of the slice: x: 4 (x_hi: 2, x_lo: 2; x = x_hi * 2 + x_lo), y: 4, z: 8, core: 2. Of those that a mesh axis runs over, the one named last changes fastest.
Arguments:
- queries: bfloat16 [2, 4096, 32, 128], P(None, 'blk', 'head'), may hold values from -30 to 30
- new_keys: bfloat16 [2, 4096, 16, 128], P(None, 'blk', 'head'), may hold values from -30 to 30
- new_values: bfloat16 [2, 4096, 16, 128], P(None, 'blk', 'head'), may hold values from -6 to 6
- pool_keys: bfloat16 [64, 128, 16, 128], P('blk', None, 'head'), may hold values from -30 to 30
- pool_values: bfloat16 [64, 128, 16, 128], P('blk', None, 'head'), may hold values from -6 to 6
- page_table: int32 [2, 32], replicated, may hold values from 0 to 63, as said below
- cache_len: int32 [2], replicated, may hold values from 1024 to 4096, as said below
- out_weight: bfloat16 [32, 128, 4608], P('head'), may hold values from -0.09375 to 0.09375
- residual: bfloat16 [2, 4096, 4608], P(None, ('blk', 'head')), may hold values from -6 to 6
- post_gain: float32 [4608], replicated, may hold values from 0.1 to 1.9
Outputs:
- mixed: bfloat16 [2, 4096, 4608], P(None, ('blk', 'head'))
Inputs may be any that keep to these rules, and one draw needn't show every extreme that they name: `page_table`: every pool page appears exactly once in the table. `cache_len`: one request has exactly 4096 cached tokens.
All inputs are finite; a program needn't handle non-finite values.
Results may differ from a plain program's by a relative error of at most 0.015.
Values may be sent and summed in bfloat16 or wider, within the bound.
A program may use at most 128 MiB of HBM per device.

v0:
```python
import jax
import jax.numpy as jnp
from jax import lax
from jax.sharding import PartitionSpec as P

soft_cap = 50.0
score_scale = 144.0 ** (-0.5)
norm_eps = 1e-06


def group_pages(page_count, page_len):
    width = max(1, min(page_count, 2048 // page_len))
    while page_count % width:
        width -= 1
    return width


def attend_pages(running, grouped, key_pages, value_pages, valid_keys):
    page_count, page_len, kv_heads, head_dim = key_pages.shape
    tok_rows = valid_keys.shape[1]
    width = group_pages(page_count, page_len)
    groups = page_count // width
    key_groups = key_pages.reshape(groups, width * page_len, kv_heads, head_dim)
    value_groups = value_pages.reshape(groups, width * page_len, kv_heads, head_dim)
    valid_groups = (
        valid_keys.reshape(groups, width, tok_rows, page_len)
        .transpose(0, 2, 1, 3)
        .reshape(groups, tok_rows, width * page_len)
    )

    def compute(carry_in, key_block, value_block, valid_block):
        numerator, denominator = carry_in
        scores = (
            jnp.einsum("tkgd,skd->kgts", grouped, key_block, preferred_element_type=jnp.float32)
            * score_scale
        )
        capped = soft_cap * jnp.tanh(scores / soft_cap)
        weights = jnp.where(valid_block[None, None], jnp.exp(capped), 0.0).astype(jnp.bfloat16)
        numerator = numerator + jnp.einsum(
            "kgts,skd->tkgd", weights, value_block, preferred_element_type=jnp.float32
        )
        denominator = denominator + jnp.sum(weights.astype(jnp.float32), axis=-1)
        return (numerator, denominator)

    def one_group(carry_in, inputs):
        key_block, value_block, valid_block = inputs
        carry_out = compute(carry_in, key_block, value_block, valid_block)
        return (carry_out, None)

    result, _ = lax.scan(one_group, running, (key_groups, value_groups, valid_groups))
    return result


def shards(
    queries,
    new_keys,
    new_values,
    pool_keys,
    pool_values,
    page_table,
    cache_len,
    out_weight,
    residual,
    post_gain,
):
    req_count, per_req, heads_here, head_dim = queries.shape
    tok_dev = req_count * per_req
    kv_here = new_keys.shape[2]
    page_len = pool_keys.shape[1]
    slot_count = page_table.shape[1]
    blk_place = lax.axis_index("blk")
    row_ids = jnp.arange(tok_dev, dtype=jnp.int32)
    row_request = row_ids // per_req
    row_offset = blk_place * per_req + row_ids % per_req
    grouped = queries.reshape(tok_dev, kv_here, heads_here // kv_here, head_dim)
    page_rows = jnp.arange(page_len, dtype=jnp.int32)
    request_ids = jnp.arange(req_count, dtype=jnp.int32)
    row_onehot = row_request[:, None] == request_ids[None, :]
    start_carry = (
        jnp.zeros((tok_dev, kv_here, heads_here // kv_here, head_dim), jnp.float32),
        jnp.zeros((kv_here, heads_here // kv_here, tok_dev), jnp.float32),
    )
    pieces = (
        lax.all_gather(pool_keys, "blk", axis=0, tiled=True),
        lax.all_gather(pool_values, "blk", axis=0, tiled=True),
    )
    page_ids = jnp.arange(pieces[0].shape[0], dtype=jnp.int32)
    matches = page_ids[:, None, None] == page_table[None, :, :]
    slot_index = jnp.sum(
        jnp.where(matches, jnp.arange(slot_count, dtype=jnp.int32)[None, None, :], 0), axis=2
    )
    owned_page = jnp.any(matches, axis=2)
    position = slot_index[:, :, None] * page_len + page_rows[None, None, :]
    keep_keys = owned_page[:, :, None] & (position < cache_len[None, :, None])
    running = attend_pages(
        start_carry,
        grouped,
        pieces[0],
        pieces[1],
        jnp.any(keep_keys[:, None, :, :] & row_onehot[None, :, :, None], axis=2),
    )
    pieces = (
        lax.all_gather(new_keys, "blk", axis=1, tiled=True),
        lax.all_gather(new_values, "blk", axis=1, tiled=True),
    )
    piece_pages = pieces[0].shape[1] // page_len
    page_index = jnp.arange(req_count * piece_pages, dtype=jnp.int32)
    firsts = page_index % piece_pages * page_len
    key_pages = pieces[0].reshape(req_count * piece_pages, page_len, kv_here, head_dim)
    value_pages = pieces[1].reshape(req_count * piece_pages, page_len, kv_here, head_dim)
    offsets = firsts[:, None] + page_rows[None, :]
    same_request = (page_index // piece_pages)[:, None] == row_request[None, :]
    running = attend_pages(
        running,
        grouped,
        key_pages,
        value_pages,
        same_request[:, :, None] & (offsets[:, None, :] <= row_offset[None, :, None]),
    )
    numerator, denominator = running
    attended = (numerator / jnp.transpose(denominator, (2, 0, 1))[..., None]).astype(jnp.bfloat16)
    head_count = lax.axis_size("head")
    share = per_req // head_count
    feature_len = heads_here * head_dim
    attended = (
        attended.reshape(req_count, head_count, share, feature_len)
        .transpose(1, 0, 2, 3)
        .reshape(tok_dev, feature_len)
    )
    weight_rows = out_weight.reshape(feature_len, out_weight.shape[2])
    projected = lax.psum_scatter(
        jnp.dot(attended, weight_rows, preferred_element_type=jnp.float32).astype(jnp.bfloat16),
        "head",
        scatter_dimension=0,
        tiled=True,
    ).astype(jnp.float32)
    projected = projected.reshape(req_count, share, projected.shape[1])
    inv_rms = lax.rsqrt(jnp.mean(projected * projected, axis=-1, keepdims=True) + norm_eps)
    mixed_out = residual.astype(jnp.float32) + post_gain * projected * inv_rms
    return mixed_out.astype(jnp.bfloat16)


def solution(mesh):
    placed = (
        P(None, "blk", "head", None),
        P(None, "blk", "head", None),
        P(None, "blk", "head", None),
        P("blk", None, "head", None),
        P("blk", None, "head", None),
        P(),
        P(),
        P("head", None, None),
        P(None, ("blk", "head"), None),
        P(),
    )
    return jax.shard_map(
        shards,
        mesh=mesh,
        in_specs=placed,
        out_specs=P(None, ("blk", "head"), None),
        check_vma=False,
    )
```

profile of v0, /device:TPU:32, one launch (start us, length us, event | category | flops | bytes accessed | tf_op | source)
XLA Modules:
  0.0 406.5 jit_solution(9550354351666353231)
XLA Ops:
  6.5 0.0 all-gather.7.cloned.1.call-start
  6.5 1.6 copy.33
  8.1 0.0 all-gather.7.cloned.1.call-update
  8.2 0.0 all-gather.5.cloned.1.call-start
  8.2 1.6 copy.29
  9.8 0.0 all-gather.5.cloned.1.call-update
  9.8 0.0 all-gather.9.cloned.1.call-start
  9.9 1.6 copy.37
  11.5 0.0 all-gather.9.cloned.1.call-update
  11.5 0.0 all-gather.11.cloned.1.call-start
  11.5 1.6 copy.38
  13.1 0.0 all-gather.11.cloned.1.call-update
  13.1 0.0 reduce-scatter.2.cloned.1.call-start
  13.2 0.8 select_reduce_fusion
  14.0 0.1 copy.31
  14.1 0.8 fusion.16
  14.9 0.1 copy.30
  15.0 0.9 compare_and_fusion
  15.9 3.5 and_reduce_fusion
  19.4 4.8 %copy.32 = pred[4,256,16,128]{1,3,2,0:T(8,128)(4,1)} copy(pred[4,256,16,128]{3,1,2,0:T(8,128)(4,1)S(1)} %bitcast.108) | data formatting | bytes 4194304 | tf_op jit(solution)/shard_map/transpose | solution.py:27
  24.3 0.1 broadcast_compare_fusion
  24.4 0.1 broadcast_bitcast_fusion
  24.5 1.7 bitcast_and_fusion
  26.2 51.5 %all-gather.7.cloned.1.call-done = bf16[64,128,2,128]{3,1,0,2:T(8,128)(2,1)} async-done(((bf16[2,128,2,128]{3,1,0,2:T(8,128)(2,1)}), bf16[64,128,2,128]{3,1,0,2:T(8,128)(2,1)}) %all-gather.7.cloned.1.call-update) | async-done | bytes 4194320 | tf_op jit(solution)/shard_map/all_gather | solution.py:84
  77.7 68.5 %all-gather.5.cloned.1.call-done = bf16[64,128,2,128]{3,1,0,2:T(8,128)(2,1)} async-done(((bf16[2,128,2,128]{3,1,0,2:T(8,128)(2,1)}), bf16[64,128,2,128]{3,1,0,2:T(8,128)(2,1)}) %all-gather.5.cloned.1.call-update) | async-done | bytes 4194320 | tf_op jit(solution)/shard_map/all_gather | solution.py:85
  146.3 41.6 %while.30 = (s32[]{:T(128)}, f32[256,2,2,128]{0,3,2,1:T(8,128)S(1)}, f32[2,2,256]{2,1,0:T(2,128)S(1)}, bf16[4,2048,2,128]{3,1,0,2:T(8,128)(2,1)}, pred[4,256,204...) while((s32[]{:T(128)}, ...), condition=%wide.region_5.6_spmd.clone, body=%wide.region_3.5_spmd.clone.sunk | while | flops 1086587904 | bytes 13386860 | solution.py:50
  146.3 1.2 dynamic-slice_bitcast_fusion.5
  147.5 5.7 %convert_reduce_fusion.5 = (f32[2,2,256]{2,1,0:T(2,128)S(1)}, bf16[2,2,256,2048]{2,3,1,0:T(8,128)(2,1)}) fusion(bf16[256,2,2,128]{3,0,2,1:T(8,128)(2,1)S(1)} %get-tuple-element.391, bf16[4,2048,2,128]{3,1,0,2:T(8,128)(2,1)} %get-tuple-element.390, s32[]{:T(128)} %get-tuple-element.376, pred[256,2048]{0,1:T(8,128)(4,1)S(1)} %dynamic-slice_bitcast_fusion.5), kind=kOutput, calls=%fused_computation.14.clone.1 | convolution fusion | flops 549452800 | bytes 6033920 | tf_op jit(solution)/shard_map/while/body/eval_jaxpr/tkgd,skd->kgts/dot_general | solution.py:34
  153.2 3.4 fusion.47
  156.6 1.2 dynamic-slice_bitcast_fusion.5
  157.9 5.7 %convert_reduce_fusion.5 = (f32[2,2,256]{2,1,0:T(2,128)S(1)}, bf16[2,2,256,2048]{2,3,1,0:T(8,128)(2,1)}) fusion(bf16[256,2,2,128]{3,0,2,1:T(8,128)(2,1)S(1)} %get-tuple-element.391, bf16[4,2048,2,128]{3,1,0,2:T(8,128)(2,1)} %get-tuple-element.390, s32[]{:T(128)} %get-tuple-element.376, pred[256,2048]{0,1:T(8,128)(4,1)S(1)} %dynamic-slice_bitcast_fusion.5), kind=kOutput, calls=%fused_computation.14.clone.1 | convolution fusion | flops 549452800 | bytes 6033920 | tf_op jit(solution)/shard_map/while/body/eval_jaxpr/tkgd,skd->kgts/dot_general | solution.py:34
  163.5 3.5 fusion.47
  167.0 1.2 dynamic-slice_bitcast_fusion.5
  168.3 5.7 %convert_reduce_fusion.5 = (f32[2,2,256]{2,1,0:T(2,128)S(1)}, bf16[2,2,256,2048]{2,3,1,0:T(8,128)(2,1)}) fusion(bf16[256,2,2,128]{3,0,2,1:T(8,128)(2,1)S(1)} %get-tuple-element.391, bf16[4,2048,2,128]{3,1,0,2:T(8,128)(2,1)} %get-tuple-element.390, s32[]{:T(128)} %get-tuple-element.376, pred[256,2048]{0,1:T(8,128)(4,1)S(1)} %dynamic-slice_bitcast_fusion.5), kind=kOutput, calls=%fused_computation.14.clone.1 | convolution fusion | flops 549452800 | bytes 6033920 | tf_op jit(solution)/shard_map/while/body/eval_jaxpr/tkgd,skd->kgts/dot_general | solution.py:34
  173.9 3.5 fusion.47
  177.5 1.2 dynamic-slice_bitcast_fusion.5
  178.7 5.7 %convert_reduce_fusion.5 = (f32[2,2,256]{2,1,0:T(2,128)S(1)}, bf16[2,2,256,2048]{2,3,1,0:T(8,128)(2,1)}) fusion(bf16[256,2,2,128]{3,0,2,1:T(8,128)(2,1)S(1)} %get-tuple-element.391, bf16[4,2048,2,128]{3,1,0,2:T(8,128)(2,1)} %get-tuple-element.390, s32[]{:T(128)} %get-tuple-element.376, pred[256,2048]{0,1:T(8,128)(4,1)S(1)} %dynamic-slice_bitcast_fusion.5), kind=kOutput, calls=%fused_computation.14.clone.1 | convolution fusion | flops 549452800 | bytes 6033920 | tf_op jit(solution)/shard_map/while/body/eval_jaxpr/tkgd,skd->kgts/dot_general | solution.py:34
  184.4 3.5 fusion.47
  187.9 26.7 %all-gather.9.cloned.1.call-done = bf16[2,4096,2,128]{3,1,0,2:T(8,128)(2,1)} async-done(((bf16[2,128,2,128]{3,1,0,2:T(8,128)(2,1)}), bf16[2,4096,2,128]{3,1,0,2:T(8,128)(2,1)}) %all-gather.9.cloned.1.call-update) | async-done | bytes 4194320 | tf_op jit(solution)/shard_map/all_gather | solution.py:104
  214.6 68.1 %all-gather.11.cloned.1.call-done = bf16[2,4096,2,128]{3,1,0,2:T(8,128)(2,1)} async-done(((bf16[2,128,2,128]{3,1,0,2:T(8,128)(2,1)}), bf16[2,4096,2,128]{3,1,0,2:T(8,128)(2,1)}) %all-gather.11.cloned.1.call-update) | async-done | bytes 4194320 | tf_op jit(solution)/shard_map/all_gather | solution.py:103
  282.7 26.7 %while.29 = (s32[]{:T(128)}, f32[256,2,2,128]{0,3,2,1:T(8,128)S(1)}, f32[2,2,256]{2,1,0:T(2,128)S(1)}, bf16[4,2048,2,128]{3,1,0,2:T(8,128)(2,1)}, pred[4,256,204...) while((s32[]{:T(128)}, ...), condition=%wide.region_8.9_spmd, body=%wide.region_6.8_spmd.sunk | while | flops 1086455808 | bytes 13386841 | solution.py:50
  282.7 0.2 dynamic-slice_bitcast_fusion.4
  282.9 4.3 %convert_reduce_fusion.4 = (f32[2,2,256]{2,1,0:T(2,128)S(1)}, bf16[2,2,256,2048]{2,3,1,0:T(8,128)(2,1)S(1)}) fusion(bf16[256,2,2,128]{3,0,2,1:T(8,128)(2,1)S(1)} %get-tuple-element.416, bf16[4,2048,2,128]{3,1,0,2:T(8,128)(2,1)} %get-tuple-element.415, s32[]{:T(128)} %get-tuple-element.402, pred[256,2048]{0,1:T(8,128)(4,1)S(1)} %dynamic-slice_bitcast_fusion.4), kind=kOutput, calls=%fused_computation.2.clone.1 | convolution fusion | flops 549452800 | bytes 6033920 | tf_op jit(solution)/shard_map/while/body/eval_jaxpr/tkgd,skd->kgts/dot_general | solution.py:34
  287.2 2.1 fusion.43
  289.4 0.2 dynamic-slice_bitcast_fusion.4
  289.5 4.3 %convert_reduce_fusion.4 = (f32[2,2,256]{2,1,0:T(2,128)S(1)}, bf16[2,2,256,2048]{2,3,1,0:T(8,128)(2,1)S(1)}) fusion(bf16[256,2,2,128]{3,0,2,1:T(8,128)(2,1)S(1)} %get-tuple-element.416, bf16[4,2048,2,128]{3,1,0,2:T(8,128)(2,1)} %get-tuple-element.415, s32[]{:T(128)} %get-tuple-element.402, pred[256,2048]{0,1:T(8,128)(4,1)S(1)} %dynamic-slice_bitcast_fusion.4), kind=kOutput, calls=%fused_computation.2.clone.1 | convolution fusion | flops 549452800 | bytes 6033920 | tf_op jit(solution)/shard_map/while/body/eval_jaxpr/tkgd,skd->kgts/dot_general | solution.py:34
  293.9 2.1 fusion.43
  296.0 0.2 dynamic-slice_bitcast_fusion.4
  296.2 4.3 %convert_reduce_fusion.4 = (f32[2,2,256]{2,1,0:T(2,128)S(1)}, bf16[2,2,256,2048]{2,3,1,0:T(8,128)(2,1)S(1)}) fusion(bf16[256,2,2,128]{3,0,2,1:T(8,128)(2,1)S(1)} %get-tuple-element.416, bf16[4,2048,2,128]{3,1,0,2:T(8,128)(2,1)} %get-tuple-element.415, s32[]{:T(128)} %get-tuple-element.402, pred[256,2048]{0,1:T(8,128)(4,1)S(1)} %dynamic-slice_bitcast_fusion.4), kind=kOutput, calls=%fused_computation.2.clone.1 | convolution fusion | flops 549452800 | bytes 6033920 | tf_op jit(solution)/shard_map/while/body/eval_jaxpr/tkgd,skd->kgts/dot_general | solution.py:34
  300.5 2.1 fusion.43
  302.7 0.2 dynamic-slice_bitcast_fusion.4
  302.9 4.3 %convert_reduce_fusion.4 = (f32[2,2,256]{2,1,0:T(2,128)S(1)}, bf16[2,2,256,2048]{2,3,1,0:T(8,128)(2,1)S(1)}) fusion(bf16[256,2,2,128]{3,0,2,1:T(8,128)(2,1)S(1)} %get-tuple-element.416, bf16[4,2048,2,128]{3,1,0,2:T(8,128)(2,1)} %get-tuple-element.415, s32[]{:T(128)} %get-tuple-element.402, pred[256,2048]{0,1:T(8,128)(4,1)S(1)} %dynamic-slice_bitcast_fusion.4), kind=kOutput, calls=%fused_computation.2.clone.1 | convolution fusion | flops 549452800 | bytes 6033920 | tf_op jit(solution)/shard_map/while/body/eval_jaxpr/tkgd,skd->kgts/dot_general | solution.py:34
  307.2 2.1 fusion.43
  309.5 0.2 copy.41
  309.6 0.1 reshape.208
  309.8 0.0 copy-start
  309.8 0.0 copy-start.2
  309.8 5.2 %convolution_convert_fusion = bf16[256,4608]{1,0:T(8,128)(2,1)} fusion(bf16[256,512]{1,0:T(8,128)(2,1)S(1)} %bitcast.115, bf16[512,4608]{1,0:T(8,128)(2,1)} %bitcast.116), kind=kOutput, calls=%fused_computation.27 | convolution fusion | flops 1209139200 | bytes 7340032 | tf_op jit(solution)/shard_map/dot_general | solution.py:132
  315.0 0.0 reduce-scatter.2.cloned.1.call-update
  315.0 81.9 %reduce-scatter.2.cloned.1.call-done = bf16[32,4608]{1,0:T(8,128)(2,1)} async-done(((bf16[256,4608]{1,0:T(8,128)(2,1)}), bf16[32,4608]{1,0:T(8,128)(2,1)}) %reduce-scatter.2.cloned.1.call-update) | async-done | bytes 294928 | tf_op jit(solution)/shard_map/reduce_scatter | solution.py:131
  396.9 1.1 multiply_reduce_fusion
  398.0 0.1 rsqrt.12
  398.1 0.0 copy-done
  398.1 1.8 add_convert_fusion
  (25 shorter events, 0.3 us)
Async XLA Ops:
  6.5 17.7 %copy-start.1 = (bf16[2,128,4,128]{3,2,1,0:T(4,128)(2,1)S(1)}, bf16[2,128,4,128]{3,2,1,0:T(4,128)(2,1)}, u32[]{:S(2)}) copy-start(bf16[2,128,4,128]{3,2,1,0:T(4,128)(2,1)} %param.14) | copy-start | bytes 786436
  6.5 71.2 %all-gather.7.cloned.1.call-start = ((), (), s32[]{:S(2)}) async-start(), calls=%async_computation.2 | async-start | bytes 4325376 | tf_op jit(solution)/shard_map/all_gather | solution.py:84
  8.2 138.1 %all-gather.5.cloned.1.call-start = ((), (), s32[]{:S(2)}) async-start(), calls=%async_computation.1 | async-start | bytes 4325376 | tf_op jit(solution)/shard_map/all_gather | solution.py:85
  9.8 204.8 %all-gather.9.cloned.1.call-start = ((), (), s32[]{:S(2)}) async-start(), calls=%async_computation.3 | async-start | bytes 4325376 | tf_op jit(solution)/shard_map/all_gather | solution.py:104
  11.5 271.2 %all-gather.11.cloned.1.call-start = ((), (), s32[]{:S(2)}) async-start(), calls=%async_computation.4 | async-start | bytes 4325376 | tf_op jit(solution)/shard_map/all_gather | solution.py:103
  13.1 383.8 %reduce-scatter.2.cloned.1.call-start = ((), (), s32[]{:S(2)}) async-start(), calls=%async_computation.5 | async-start | bytes 2654208 | tf_op jit(solution)/shard_map/reduce_scatter | solution.py:131
  309.8 88.4 %copy-start = (bf16[2,16,4608]{2,1,0:T(8,128)(2,1)S(1)}, bf16[2,16,4608]{2,1,0:T(8,128)(2,1)}, u32[]{:S(2)}) copy-start(bf16[2,16,4608]{2,1,0:T(8,128)(2,1)} %param.22) | copy-start | bytes 884740
  309.8 88.3 %copy-start.2 = (f32[4608]{0:T(1024)S(1)}, f32[4608]{0:T(1024)}, u32[]{:S(2)}) copy-start(f32[4608]{0:T(1024)} %param.23) | copy-start | bytes 55300
Sparse Core Ops, SparseCore 0:
  9.2 68.4 all-gather.6
  79.6 66.6 all-gather.4
  148.2 66.3 all-gather.8
  216.3 66.3 all-gather.10
  315.1 81.7 reduce-scatter.1
where the time goes:
time: 407 us; the launch traced here: 406 us
  waiting for transfers between devices  297 us (73%)
  matrix products  67.5 us (17%)
  local copies, waits for them, and re-layouts  17.6 us (4%)
  between operations  13.3 us (3%)
  other arithmetic  10.9 us (3%)
    reduce_scatter x1, waiting for transfers between devices, shards(): lax.psum_scatter(jnp.dot(attended, weight_rows, preferred_element_type=jn...  81.9 us
    all_gather x1, waiting for transfers between devices, shards(): lax.all_gather(pool_values, 'blk', axis=0, tiled=True)  68.5 us
    all_gather x1, waiting for transfers between devices, shards(): lax.all_gather(new_keys, 'blk', axis=1, tiled=True)  68.1 us
    all_gather x1, waiting for transfers between devices, shards(): lax.all_gather(pool_keys, 'blk', axis=0, tiled=True)  51.5 us
    dot_general x8, matrix products, compute(): jnp.einsum('tkgd,skd->kgts', grouped, key_block, preferred_element_type=j...  39.8 us
    all_gather x1, waiting for transfers between devices, shards(): lax.all_gather(new_values, 'blk', axis=1, tiled=True)  26.7 us
    dot_general x8, matrix products, compute(): jnp.einsum('kgts,skd->tkgd', weights, value_block, preferred_element_type...  22.4 us
  transfers between devices with their start and end apart: 5, of which 5 were waited for; matrix products, arithmetic and copies ran while one was open for 15% of the time, Pallas kernels for 0%

commit v1 on v0

v1 whole, which is shorter than its diff:
```python
import functools

import jax
import jax.numpy as jnp
from jax import lax
from jax.experimental import pallas as pl
from jax.experimental.pallas import tpu as pltpu
from jax.sharding import PartitionSpec as P

soft_cap = 50.0
score_scale = 144.0 ** (-0.5)
norm_eps = 1e-06

MESH_ID = pl.DeviceIdType.MESH


def attend_kernel(
    zs_n,
    tok,
    kv_hbm,
    q_hbm,
    mask_ref,
    out_ref,
    kvbuf,
    qall,
    acc,
    att_send,
    att_recv,
    local_sem,
    send_sem,
    recv_sem,
    x_send,
    x_recv,
):
    blk = lax.axis_index("blk")
    me_c = lax.rem(blk, 2)
    me_z = lax.rem(blk // 2, zs_n)
    me_x = blk // (2 * zs_n)

    def place(x, z, c):
        return {"blk": (x * zs_n + z) * 2 + c}

    right = place(me_x, lax.rem(me_z + 1, zs_n), me_c)
    left = place(me_x, lax.rem(me_z + zs_n - 1, zs_n), me_c)
    sibling = place(me_x, me_z, 1 - me_c)
    partner = place(1 - me_x, me_z, me_c)

    barrier = pltpu.get_barrier_semaphore()
    for other in (right, left, sibling, partner):
        pl.semaphore_signal(barrier, inc=1, device_id=other, device_id_type=MESH_ID)

    own_kv = pltpu.make_async_copy(kv_hbm.at[me_x], kvbuf.at[me_c, me_x, me_z], local_sem.at[0])
    own_q = pltpu.make_async_copy(q_hbm.at[me_x], qall.at[me_x], local_sem.at[1])
    own_kv.start()
    own_q.start()
    pl.semaphore_wait(barrier, 4)

    q_swap = pltpu.make_async_remote_copy(
        src_ref=q_hbm.at[1 - me_x],
        dst_ref=qall.at[me_x],
        send_sem=x_send.at[0],
        recv_sem=x_recv.at[0],
        device_id=partner,
        device_id_type=MESH_ID,
    )
    kv_swap = pltpu.make_async_remote_copy(
        src_ref=kv_hbm.at[1 - me_x],
        dst_ref=kvbuf.at[me_c, me_x, me_z],
        send_sem=x_send.at[1],
        recv_sem=recv_sem.at[me_c, me_x, me_z],
        device_id=partner,
        device_id_type=MESH_ID,
    )
    q_swap.start()
    kv_swap.start()

    def forward(way, device, x, z):
        return pltpu.make_async_remote_copy(
            src_ref=kvbuf.at[me_c, x, z],
            dst_ref=kvbuf.at[me_c, x, z],
            send_sem=send_sem.at[way, x, z],
            recv_sem=recv_sem.at[me_c, x, z],
            device_id=device,
            device_id_type=MESH_ID,
        )

    def landed(c, x, z):
        pltpu.make_async_remote_copy(
            src_ref=kvbuf.at[c, x, z],
            dst_ref=kvbuf.at[c, x, z],
            send_sem=x_send.at[1],
            recv_sem=recv_sem.at[c, x, z],
            device_id=sibling,
            device_id_type=MESH_ID,
        ).wait_recv()

    half = zs_n // 2
    last = zs_n

    def steps_right(k):
        is_b = (lax.rem(k, 2) == 0) & (k > 0)
        dist = jnp.where(lax.rem(k, 2) == 1, (k + 1) // 2, jnp.maximum(k - 2, 0) // 2)
        x = jnp.where(is_b, 1 - me_x, me_x)
        return x, lax.rem(me_z - dist + zs_n, zs_n)

    def steps_left(k):
        is_b = ((lax.rem(k, 2) == 0) & (k > 0)) | (k == last - 1)
        dist = jnp.where(lax.rem(k, 2) == 1, (k + 1) // 2, jnp.maximum(k - 2, 0) // 2)
        dist = jnp.where(k >= last - 1, k - (last - half), dist)
        x = jnp.where(is_b, 1 - me_x, me_x)
        return x, lax.rem(me_z + dist, zs_n)

    def goes_right(k):
        return k <= last - 2

    def goes_left(k):
        return (k != last - 3) & (k != last)

    def is_own(k):
        return (k == 0) | (k == 2)

    rows = 2 * tok
    lane = lax.broadcasted_iota(jnp.int32, (rows, tok), 1)
    row = lax.broadcasted_iota(jnp.int32, (rows, tok), 0)
    ahead = lax.rem(row, tok) - lane

    def weigh(scores):
        capped = jnp.tanh(scores * (score_scale / soft_cap)) * soft_cap
        return jnp.exp(capped)

    ones = jnp.ones((3 * tok, 128), jnp.bfloat16)

    def dots(a, b):
        return lax.dot_general(
            a, b, (((1,), (1,)), ((), ())), preferred_element_type=jnp.float32
        )

    def attend(c, x, z):
        key_block = (x * zs_n + z) * 2 + c
        seen = mask_ref[key_block]
        for r in range(2):
            pool = pl.ds(tok, 2 * tok)
            new = pl.ds(r * 3 * tok, tok)
            every = pl.ds(r * tok, 3 * tok)
            pool_k = kvbuf[c, x, z, 0, pool, :]
            new_k = kvbuf[c, x, z, 0, new, :]
            values = jnp.concatenate([kvbuf[c, x, z, 1, every, :], ones], axis=1)
            for qx in range(2):
                query = qall[qx, r]
                query_block = (qx * zs_n + me_z) * 2 + me_c
                w_pool = weigh(dots(query, pool_k)) * seen[r : r + 1, :]
                w_new = jnp.where(
                    ahead >= (key_block - query_block) * tok, weigh(dots(query, new_k)), 0.0
                )
                both = [w_new, w_pool] if r == 0 else [w_pool, w_new]
                weights = jnp.concatenate(both, axis=1).astype(jnp.bfloat16)
                acc[qx, r] += jnp.dot(weights, values, preferred_element_type=jnp.float32)

    own_kv.wait()
    acc[...] = jnp.zeros_like(acc)

    def one_step(k, carry):
        rx, rz = steps_right(k)
        lx, lz = steps_left(k)
        own = is_own(k)

        @pl.when(k > 0)
        def _():
            landed(me_c, rx, rz)

        @pl.when(goes_right(k))
        def _():
            forward(0, right, rx, rz).start()

        @pl.when(jnp.logical_not(own))
        def _():
            landed(me_c, lx, lz)

        @pl.when(goes_left(k))
        def _():
            forward(1, left, lx, lz).start()

        forward(2, sibling, rx, rz).start()

        @pl.when(jnp.logical_not(own))
        def _():
            forward(2, sibling, lx, lz).start()

        @pl.when(k == 0)
        def _():
            own_q.wait()
            q_swap.wait_recv()

        def one_shard(i, carry):
            c = jnp.where(i % 2 == 0, me_c, 1 - me_c)
            x = jnp.where(i < 2, rx, lx)
            z = jnp.where(i < 2, rz, lz)

            @pl.when(i % 2 == 1)
            def _():
                landed(c, x, z)

            attend(c, x, z)
            return carry

        lax.fori_loop(0, jnp.where(own, 2, 4), one_shard, 0)
        return carry

    lax.fori_loop(0, last + 1, one_step, 0)

    def finished(qx, r):
        total = acc[qx, r]
        return (total[:, :128] / total[:, 128:]).astype(jnp.bfloat16)

    for r in range(2):
        att_send[r] = finished(1 - me_x, r)
    att_swap = pltpu.make_async_remote_copy(
        src_ref=att_send,
        dst_ref=att_recv,
        send_sem=x_send.at[2],
        recv_sem=x_recv.at[1],
        device_id=partner,
        device_id_type=MESH_ID,
    )
    att_swap.start()

    share = tok // 8

    def put(x, r, value):
        for g in range(2):
            columns = pl.ds(pl.multiple_of((2 * x + g) * 128, 128), 128)
            out_ref[:, r, :, columns] = value[g * tok : (g + 1) * tok].reshape(8, share, 128)

    for r in range(2):
        put(me_x, r, finished(me_x, r))
    att_swap.wait()
    for r in range(2):
        put(1 - me_x, r, att_recv[r])

    q_swap.wait_send()
    kv_swap.wait_send()

    def drain(k, carry):
        rx, rz = steps_right(k)
        lx, lz = steps_left(k)

        @pl.when(goes_right(k))
        def _():
            forward(0, right, rx, rz).wait_send()

        @pl.when(goes_left(k))
        def _():
            forward(1, left, lx, lz).wait_send()

        forward(2, sibling, rx, rz).wait_send()

        @pl.when(jnp.logical_not(is_own(k)))
        def _():
            forward(2, sibling, lx, lz).wait_send()

        return carry

    lax.fori_loop(0, last + 1, drain, 0)


def gather_and_attend(queries, new_keys, new_values, pool_keys, pool_values, page_table, cache_len):
    req, tok, heads, dim = queries.shape
    kv_heads = new_keys.shape[2]
    zs_n = lax.axis_size("blk") // 4

    def laid(new, pool):
        new = new.transpose(2, 0, 1, 3)
        pool = pool.transpose(2, 0, 1, 3).reshape(kv_heads, 2 * tok, dim)
        return jnp.concatenate([new[:, 0], pool, new[:, 1]], axis=1)

    kv = jnp.stack([laid(new_keys, pool_keys), laid(new_values, pool_values)], axis=1)
    q = queries.reshape(req, tok, kv_heads, heads // kv_heads, dim)
    q = q.transpose(2, 0, 3, 1, 4).reshape(kv_heads, req, 2 * tok, dim)

    pages = 2 * lax.axis_size("blk")
    slots = page_table.shape[1]
    match = jnp.arange(pages, dtype=jnp.int32)[:, None, None] == page_table[None]
    slot = jnp.sum(jnp.where(match, jnp.arange(slots, dtype=jnp.int32), 0), axis=2)
    owned = jnp.any(match, axis=2)
    position = slot[:, :, None] * tok + jnp.arange(tok, dtype=jnp.int32)
    seen = (owned[:, :, None] & (position < cache_len[None, :, None])).astype(jnp.float32)
    seen = seen.reshape(pages // 2, 2, req, tok).transpose(0, 2, 1, 3)
    seen = seen.reshape(pages // 2, req, 2 * tok)

    hbm = pl.BlockSpec(memory_space=pl.ANY)
    vmem = pl.BlockSpec(memory_space=pltpu.VMEM)
    return pl.pallas_call(
        functools.partial(attend_kernel, zs_n, tok),
        name="gather_and_attend",
        out_shape=jax.ShapeDtypeStruct((8, req, tok // 8, heads * dim), jnp.bfloat16),
        in_specs=[hbm, hbm, vmem],
        out_specs=vmem,
        scratch_shapes=[
            pltpu.VMEM((2, 2, zs_n, 2, 4 * tok, dim), jnp.bfloat16),
            pltpu.VMEM((2, req, 2 * tok, dim), jnp.bfloat16),
            pltpu.VMEM((2, req, 2 * tok, 2 * dim), jnp.float32),
            pltpu.VMEM((req, 2 * tok, dim), jnp.bfloat16),
            pltpu.VMEM((req, 2 * tok, dim), jnp.bfloat16),
            pltpu.SemaphoreType.DMA((2,)),
            pltpu.SemaphoreType.DMA((3, 2, zs_n)),
            pltpu.SemaphoreType.DMA((2, 2, zs_n)),
            pltpu.SemaphoreType.DMA((3,)),
            pltpu.SemaphoreType.DMA((2,)),
        ],
        compiler_params=pltpu.CompilerParams(collective_id=0, has_side_effects=True),
    )(kv, q, seen)


def shards(
    queries,
    new_keys,
    new_values,
    pool_keys,
    pool_values,
    page_table,
    cache_len,
    out_weight,
    residual,
    post_gain,
):
    req, tok, heads, dim = queries.shape
    attended = gather_and_attend(
        queries, new_keys, new_values, pool_keys, pool_values, page_table, cache_len
    )
    share = tok // lax.axis_size("head")
    attended = attended.reshape(req * tok, heads * dim)
    weight_rows = out_weight.reshape(heads * dim, out_weight.shape[2])
    projected = lax.psum_scatter(
        jnp.dot(attended, weight_rows, preferred_element_type=jnp.float32).astype(jnp.bfloat16),
        "head",
        scatter_dimension=0,
        tiled=True,
    ).astype(jnp.float32)
    projected = projected.reshape(req, share, projected.shape[1])
    inv_rms = lax.rsqrt(jnp.mean(projected * projected, axis=-1, keepdims=True) + norm_eps)
    mixed_out = residual.astype(jnp.float32) + post_gain * projected * inv_rms
    return mixed_out.astype(jnp.bfloat16)


def solution(mesh):
    placed = (
        P(None, "blk", "head", None),
        P(None, "blk", "head", None),
        P(None, "blk", "head", None),
        P("blk", None, "head", None),
        P("blk", None, "head", None),
        P(),
        P(),
        P("head", None, None),
        P(None, ("blk", "head"), None),
        P(),
    )
    return jax.shard_map(
        shards,
        mesh=mesh,
        in_specs=placed,
        out_specs=P(None, ("blk", "head"), None),
        check_vma=False,
    )
```

time: 407 us -> 175 us (0.43)
  waiting for transfers between devices: 297 us -> 79.5 us
  Pallas kernels: 0 us -> 63.5 us
  matrix products: 67.5 us -> 5.27 us
  local copies, waits for them, and re-layouts: 17.6 us -> 6.15 us
  other arithmetic: 10.9 us -> 6.75 us
    all_gather x4 -> x0, waiting for transfers between devices: 215 us -> none  [the longest x1 68.5 us: shards(): lax.all_gather(pool_values, 'blk', axis=0, tiled=True)]
    pallas_call x0 -> x1, Pallas kernels: none -> 63.5 us  [gather_and_attend(): pl.pallas_call(functools.partial(attend_kernel, zs_n, tok), name='gather_...]
    dot_general x16 -> x0, matrix products: 62.3 us -> none  [the longest x8 39.8 us: compute(): jnp.einsum('tkgd,skd->kgts', grouped, key_block, preferred_element_type=j...]
    broadcast_in_dim x8 -> x0, local copies, waits for them, and re-layouts: 5.67 us -> none  [compute(): jnp.where(valid_block[None, None], jnp.exp(capped), 0.0)]
    unnamed x12 -> x6, local copies, waits for them, and re-layouts: 6.48 us -> 1.86 us
  transfers between devices with their start and end apart: 5 -> 1, of which waited for: 5 -> 1; matrix products, arithmetic and copies ran while one was open for 15% -> 0% of each run, Pallas kernels for 0% -> 0%
where the time goes in v1:
time: 175 us
  waiting for transfers between devices  79.5 us (45%)
  Pallas kernels  63.5 us (36%)
  between operations  13.5 us (8%)
  other arithmetic  6.75 us (4%)
  local copies, waits for them, and re-layouts  6.15 us (4%)
  matrix products  5.27 us (3%)
    reduce_scatter x1, waiting for transfers between devices, shards(): lax.psum_scatter(jnp.dot(attended, weight_rows, preferred_element_type=jn...  79.5 us
    pallas_call x1, Pallas kernels, gather_and_attend(): pl.pallas_call(functools.partial(attend_kernel, zs_n, tok), name='gather_...  63.5 us
    dot_general x1, matrix products, shards(): jnp.dot(attended, weight_rows, preferred_element_type=jnp.float32)  5.27 us
  transfers between devices with their start and end apart: 1, of which 1 were waited for; matrix products, arithmetic and copies ran while one was open for 0% of the time, Pallas kernels for 0%

profile of v1, /device:TPU:32, one launch (start us, length us, event | category | flops | bytes accessed | tf_op | source)
XLA Modules:
  0.0 174.6 jit_solution(781268570978563235)
XLA Ops:
  6.5 0.0 reduce-scatter.2.cloned.1.call-start
  6.5 0.8 fusion.1
  7.3 0.8 select_reduce_fusion
  8.1 0.1 and.17
  8.2 0.1 and.19
  8.4 0.1 and.20
  8.4 0.1 mul.37
  8.6 0.1 add.42
  8.7 0.1 add.43
  8.8 0.9 copy.46
  9.7 0.9 copy.45
  10.7 0.9 copy.33
  11.6 0.9 copy.35
  12.5 1.7 copy.36
  14.3 0.8 pad_maximum_fusion.kv_hbm
  15.1 1.4 fusion.mask_ref
  16.5 63.5 %gather_and_attend.1 = bf16[8,2,16,512]{3,2,1,0:T(8,128)(2,1)} custom-call(bf16[2,2,512,128]{3,2,1,0:T(8,128)(2,1)} %pad_maximum_fusion.kv_hbm, bf16[2,2,256,128]{3,2,1,0:T(8,128)(2,1)} %bitcast.43, f32[32,2,256]{2,1,0:T(2,128)} %fusion.mask_ref), custom_call_target="tpu_custom_call" | custom-call | tf_op jit(solution)/shard_map/gather_and_attend/pallas_call | solution.py:292
  79.9 0.0 copy-start
  79.9 0.0 copy-start.1
  80.0 5.3 %convolution_convert_fusion = bf16[256,4608]{1,0:T(8,128)(2,1)} fusion(bf16[256,512]{1,0:T(8,128)(2,1)} %bitcast.48, bf16[512,4608]{1,0:T(8,128)(2,1)} %bitcast.54), kind=kOutput, calls=%fused_computation | convolution fusion | flops 1209139200 | bytes 7340032 | tf_op jit(solution)/shard_map/dot_general | solution.py:334
  85.2 0.0 reduce-scatter.2.cloned.1.call-update
  85.2 79.5 %reduce-scatter.2.cloned.1.call-done = bf16[32,4608]{1,0:T(8,128)(2,1)} async-done(((bf16[256,4608]{1,0:T(8,128)(2,1)}), bf16[32,4608]{1,0:T(8,128)(2,1)}) %reduce-scatter.2.cloned.1.call-update) | async-done | bytes 294928 | tf_op jit(solution)/shard_map/reduce_scatter | solution.py:333
  164.7 1.1 multiply_reduce_fusion
  165.9 0.1 rsqrt.12
  165.9 0.0 copy-done
  165.9 0.0 copy-done.1
  165.9 1.8 %add_convert_fusion = bf16[2,16,4608]{2,1,0:T(8,128)(2,1)} fusion(bf16[2,16,4608]{2,1,0:T(8,128)(2,1)S(1)} %copy-done, f32[2,16]{1,0:T(2,128)S(1)} %rsqrt.12, f32[4608]{0:T(1024)S(1)} %copy-done.1, bf16[2,16,4608]{2,1,0:T(8,128)(2,1)} %bitcast.42), kind=kLoop, calls=%fused_computation.1 | loop fusion | flops 884736 | bytes 903296 | tf_op jit(solution)/shard_map/convert_element_type | solution.py:342
  (7 shorter events, 0.1 us)
Async XLA Ops:
  6.5 158.2 %reduce-scatter.2.cloned.1.call-start = ((), (), s32[]{:S(2)}) async-start(), calls=%async_computation.1 | async-start | bytes 2654208 | tf_op jit(solution)/shard_map/reduce_scatter | solution.py:333
  79.9 86.0 %copy-start = (bf16[2,16,4608]{2,1,0:T(8,128)(2,1)S(1)}, bf16[2,16,4608]{2,1,0:T(8,128)(2,1)}, u32[]{:S(2)}) copy-start(bf16[2,16,4608]{2,1,0:T(8,128)(2,1)} %param.18) | copy-start | bytes 884740
  79.9 86.0 %copy-start.1 = (f32[4608]{0:T(1024)S(1)}, f32[4608]{0:T(1024)}, u32[]{:S(2)}) copy-start(f32[4608]{0:T(1024)} %param.19) | copy-start | bytes 55300
Sparse Core Ops, SparseCore 0:
  85.4 79.3 reduce-scatter.1

commit v2 on v1

--- a/solution.py
+++ b/solution.py
@@ -311,6 +311,115 @@
     )(kv, q, seen)
 
 
+def project_kernel(
+    att_ref, weight_hbm, residual_ref, gain_ref, out_ref, weight, part, got, total, w_sem, send_sem, recv_sem
+):
+    me = lax.axis_index("head")
+    me_y, me_h = me // 2, lax.rem(me, 2)
+    thirds = 3
+    wide = part.shape[2] // thirds
+    tile = 512
+
+    def loads(t):
+        columns = pl.ds(t * wide, wide)
+        return pltpu.make_async_copy(weight_hbm.at[:, columns], weight.at[:, columns], w_sem.at[t])
+
+    for t in range(thirds):
+        loads(t).start()
+
+    peers = []
+    for dy, dh in ((1, 0), (3, 0), (0, 1), (2, 0), (1, 1), (3, 1), (2, 1)):
+        to = lax.rem(me_y + dy, 4) * 2 + lax.rem(me_h + dh, 2)
+        source = lax.rem(me_y + 4 - dy, 4) * 2 + lax.rem(me_h + dh, 2)
+        peers.append((to, source))
+
+    barrier = pltpu.get_barrier_semaphore()
+    for to, _ in peers:
+        pl.semaphore_signal(barrier, inc=1, device_id={"head": to}, device_id_type=MESH_ID)
+
+    def sends(i, t):
+        columns = pl.ds(t * wide, wide)
+        to = peers[i][0]
+        return pltpu.make_async_remote_copy(
+            src_ref=part.at[to, :, columns],
+            dst_ref=got.at[i, :, columns],
+            send_sem=send_sem.at[t, i],
+            recv_sem=recv_sem.at[t, i],
+            device_id={"head": to},
+            device_id_type=MESH_ID,
+        )
+
+    attended = att_ref[...].reshape(8 * 32, att_ref.shape[3])
+    for t in range(thirds):
+        loads(t).wait()
+
+        def one_tile(i, carry):
+            columns = pl.ds(pl.multiple_of(t * wide + i * tile, tile), tile)
+            value = jnp.dot(attended, weight[:, columns], preferred_element_type=jnp.float32)
+            part[:, :, columns] = value.astype(jnp.bfloat16).reshape(8, 32, tile)
+            return carry
+
+        lax.fori_loop(0, wide // tile, one_tile, 0)
+        if t == 0:
+            pl.semaphore_wait(barrier, 7)
+        for i in range(7):
+            sends(i, t).start()
+
+    square = jnp.zeros((32, 1), jnp.float32)
+    for t in range(thirds):
+        for i in range(7):
+            sends(i, t).wait_recv()
+
+        def add_tile(n, square):
+            columns = pl.ds(pl.multiple_of(t * wide + n * tile, tile), tile)
+            value = part[me, :, columns].astype(jnp.float32)
+            for i in range(7):
+                value = value + got[i, :, columns].astype(jnp.float32)
+            total[:, columns] = value
+            return square + jnp.sum(value * value, axis=1, keepdims=True)
+
+        square = lax.fori_loop(0, wide // tile, add_tile, square)
+
+    inv_rms = lax.rsqrt(square / part.shape[2] + norm_eps)
+
+    def mix_tile(n, carry):
+        columns = pl.ds(pl.multiple_of(n * tile, tile), tile)
+        value = gain_ref[:, columns] * total[:, columns] * inv_rms
+        for r in range(2):
+            rows = value[r * 16 : (r + 1) * 16]
+            out_ref[r, :, columns] = (residual_ref[r, :, columns].astype(jnp.float32) + rows).astype(
+                jnp.bfloat16
+            )
+        return carry
+
+    lax.fori_loop(0, part.shape[2] // tile, mix_tile, 0)
+    for t in range(thirds):
+        for i in range(7):
+            sends(i, t).wait_send()
+
+
+def project_and_mix(attended, weight_rows, residual, post_gain):
+    depth, width = weight_rows.shape
+    vmem = pl.BlockSpec(memory_space=pltpu.VMEM)
+    return pl.pallas_call(
+        project_kernel,
+        name="project_and_mix",
+        out_shape=jax.ShapeDtypeStruct(residual.shape, jnp.bfloat16),
+        in_specs=[vmem, pl.BlockSpec(memory_space=pl.ANY), vmem, vmem],
+        out_specs=vmem,
+        scratch_shapes=[
+            pltpu.VMEM((depth, width), jnp.bfloat16),
+            pltpu.VMEM((8, 32, width), jnp.bfloat16),
+            pltpu.VMEM((7, 32, width), jnp.bfloat16),
+            pltpu.VMEM((32, width), jnp.float32),
+            pltpu.SemaphoreType.DMA((3,)),
+            pltpu.SemaphoreType.DMA((3, 7)),
+            pltpu.SemaphoreType.DMA((3, 7)),
+        ],
+        compiler_params=pltpu.CompilerParams(collective_id=1, has_side_effects=True),
+    )(attended, weight_rows, residual, post_gain.reshape(1, width))
+
+
 def shards(
     queries,
     new_keys,
@@ -323,23 +432,11 @@
     residual,
     post_gain,
 ):
-    req, tok, heads, dim = queries.shape
+    heads, dim, width = out_weight.shape
     attended = gather_and_attend(
         queries, new_keys, new_values, pool_keys, pool_values, page_table, cache_len
     )
-    share = tok // lax.axis_size("head")
-    attended = attended.reshape(req * tok, heads * dim)
-    weight_rows = out_weight.reshape(heads * dim, out_weight.shape[2])
-    projected = lax.psum_scatter(
-        jnp.dot(attended, weight_rows, preferred_element_type=jnp.float32).astype(jnp.bfloat16),
-        "head",
-        scatter_dimension=0,
-        tiled=True,
-    ).astype(jnp.float32)
-    projected = projected.reshape(req, share, projected.shape[1])
-    inv_rms = lax.rsqrt(jnp.mean(projected * projected, axis=-1, keepdims=True) + norm_eps)
-    mixed_out = residual.astype(jnp.float32) + post_gain * projected * inv_rms
-    return mixed_out.astype(jnp.bfloat16)
+    return project_and_mix(attended, out_weight.reshape(heads * dim, width), residual, post_gain)
 
 
 def solution(mesh):

time: 175 us -> 113 us (0.65)
  waiting for transfers between devices: 79.5 us -> 0 us
  Pallas kernels: 63.5 us -> 99.9 us
  between operations: 13.5 us -> 0.12 us
  matrix products: 5.27 us -> 0 us
  other arithmetic: 6.75 us -> 3.8 us
  local copies, waits for them, and re-layouts: 6.15 us -> 8.38 us
    reduce_scatter x1 -> x0, waiting for transfers between devices: 79.5 us -> none  [shards(): lax.psum_scatter(jnp.dot(attended, weight_rows, preferred_element_type=jn...]
    pallas_call x0 -> x1, Pallas kernels: none -> 36.6 us  [project_and_mix(): pl.pallas_call(project_kernel, name='project_and_mix', out_shape=jax.Shap...]
    dot_general x1 -> x0, matrix products: 5.27 us -> none  [shards(): jnp.dot(attended, weight_rows, preferred_element_type=jnp.float32)]
    convert_element_type x1 -> x0, other arithmetic: 1.82 us -> none  [shards(): return mixed_out.astype(jnp.bfloat16)]
    unnamed x6 -> x5, local copies, waits for them, and re-layouts: 1.86 us -> 3.55 us
  transfers between devices with their start and end apart: 1 -> 0, of which waited for: 1 -> 0; matrix products, arithmetic and copies ran while one was open for 0% -> 0% of each run, Pallas kernels for 0% -> 0%
where the time goes in v2:
time: 113 us; the launch traced here: 112 us
  Pallas kernels  99.9 us (88%)
  local copies, waits for them, and re-layouts  8.38 us (7%)
  other arithmetic  3.8 us (3%)
    pallas_call x1, Pallas kernels, gather_and_attend(): pl.pallas_call(functools.partial(attend_kernel, zs_n, tok), name='gather_...  63.3 us
    pallas_call x1, Pallas kernels, project_and_mix(): pl.pallas_call(project_kernel, name='project_and_mix', out_shape=jax.Shap...  36.6 us
    unnamed x5, local copies, waits for them, and re-layouts  3.55 us

profile of v2, /device:TPU:32, one launch (start us, length us, event | category | flops | bytes accessed | tf_op | source)
XLA Modules:
  0.0 112.2 jit_solution(10833934847469949473)
XLA Ops:
  0.0 0.0 copy-start
  0.0 0.9 copy.46
  1.0 0.9 copy.45
  1.9 0.9 copy.33
  2.8 0.9 copy.35
  3.8 0.8 pad_maximum_fusion.kv_hbm
  4.6 0.8 select_reduce_fusion
  5.4 0.1 mul.16
  5.6 0.1 add.25
  5.7 0.1 add.26
  5.8 0.8 fusion.1
  6.6 0.1 and.17
  6.7 0.1 and.19
  6.8 0.1 and.20
  6.9 1.4 %fusion.mask_ref = f32[32,2,256]{2,1,0:T(2,128)} fusion(pred[32,2,256]{2,0,1:T(8,128)(4,1)S(1)} %and.20, s32[32,2,256]{2,1,0:T(2,128)S(1)} %add.26, s32[2]{0:T(128)} %param.16, s32[256]{0:T(256)S(1)} %iota_bitcast_fusion), kind=kLoop, calls=%fused_computation.6 | loop fusion | flops 65536 | bytes 148488 | tf_op jit(solution)/shard_map/convert_element_type | solution.py:286
  8.3 1.7 %copy.36 = bf16[2,128,2,2,128]{4,1,3,0,2:T(8,128)(2,1)} copy(bf16[2,128,2,2,128]{4,3,2,1,0:T(2,128)(2,1)} %bitcast.43) | data formatting | bytes 524288 | tf_op jit(solution)/shard_map/reshape | solution.py:277
  10.0 63.3 %gather_and_attend.1.att_ref = bf16[8,2,16,512]{3,2,1,0:T(8,128)(2,1)} custom-call(bf16[2,2,512,128]{3,2,1,0:T(8,128)(2,1)} %pad_maximum_fusion.kv_hbm, bf16[2,2,256,128]{3,2,1,0:T(8,128)(2,1)} %bitcast.38, f32[32,2,256]{2,1,0:T(2,128)} %fusion.mask_ref), custom_call_target="tpu_custom_call" | custom-call | tf_op jit(solution)/shard_map/gather_and_attend/pallas_call | solution.py:292
  73.3 0.0 copy-done
  73.3 0.6 reshape.42.gain_ref
  73.9 36.6 %project_and_mix.1 = bf16[2,16,4608]{2,1,0:T(8,128)(2,1)} custom-call(bf16[8,2,16,512]{3,2,1,0:T(8,128)(2,1)} %gather_and_attend.1.att_ref, bf16[512,4608]{1,0:T(8,128)(2,1)} %bitcast.37, bf16[2,16,4608]{2,1,0:T(8,128)(2,1)} %residual_ref.1, f32[1,4608]{1,0:T(1,128)} %reshape.42.gain_ref), custom_call_target="tpu_custom_call" | custom-call | tf_op jit(solution)/shard_map/project_and_mix/pallas_call | solution.py:404
  110.5 1.7 %copy.48 = bf16[2,16,4608]{2,1,0:T(8,128)(2,1)} copy(bf16[2,16,4608]{2,1,0:T(8,128)(2,1)} %project_and_mix.1) | data formatting | bytes 589824
  (6 shorter events, 0.1 us)
Async XLA Ops:
  0.0 73.3 %copy-start = (f32[4608]{0:T(1024)S(1)}, f32[4608]{0:T(1024)}, u32[]{:S(2)}) copy-start(f32[4608]{0:T(1024)} %param.19) | copy-start | bytes 55300

commit v3 on v2

--- a/solution.py
+++ b/solution.py
@@ -10,6 +10,7 @@
 soft_cap = 50.0
 score_scale = 144.0 ** (-0.5)
 norm_eps = 1e-06
+log2_e = 1.4426950408889634
 
 MESH_ID = pl.DeviceIdType.MESH
 
@@ -19,11 +20,14 @@
     tok,
     kv_hbm,
     q_hbm,
-    mask_ref,
+    table_ref,
+    length_ref,
     out_ref,
     kvbuf,
     qall,
     acc,
+    seen,
+    first,
     att_send,
     att_recv,
     local_sem,
@@ -63,16 +67,31 @@
         device_id=partner,
         device_id_type=MESH_ID,
     )
-    kv_swap = pltpu.make_async_remote_copy(
-        src_ref=kv_hbm.at[1 - me_x],
-        dst_ref=kvbuf.at[me_c, me_x, me_z],
-        send_sem=x_send.at[1],
-        recv_sem=recv_sem.at[me_c, me_x, me_z],
-        device_id=partner,
-        device_id_type=MESH_ID,
-    )
+
+    def kv_swap(h):
+        return pltpu.make_async_remote_copy(
+            src_ref=kv_hbm.at[1 - me_x, h],
+            dst_ref=kvbuf.at[me_c, me_x, me_z, h],
+            send_sem=x_send.at[2 + h],
+            recv_sem=x_recv.at[2 + h],
+            device_id=partner,
+            device_id_type=MESH_ID,
+        )
+
+    def kv_swap_landed(h):
+        here = kvbuf.at[me_c, 1 - me_x, me_z, h]
+        pltpu.make_async_remote_copy(
+            src_ref=here,
+            dst_ref=here,
+            send_sem=x_send.at[2 + h],
+            recv_sem=x_recv.at[2 + h],
+            device_id=partner,
+            device_id_type=MESH_ID,
+        ).wait_recv()
+
     q_swap.start()
-    kv_swap.start()
+    kv_swap(0).start()
+    kv_swap(1).start()
 
     def forward(way, device, x, z):
         return pltpu.make_async_remote_copy(
@@ -84,6 +103,16 @@
             device_id_type=MESH_ID,
         )
 
+    def forward_half(way, device, x, z, h):
+        return pltpu.make_async_remote_copy(
+            src_ref=kvbuf.at[me_c, x, z, h],
+            dst_ref=kvbuf.at[me_c, x, z, h],
+            send_sem=send_sem.at[way, x, z],
+            recv_sem=recv_sem.at[me_c, x, z],
+            device_id=device,
+            device_id_type=MESH_ID,
+        )
+
     def landed(c, x, z):
         pltpu.make_async_remote_copy(
             src_ref=kvbuf.at[c, x, z],
@@ -94,30 +123,40 @@
             device_id_type=MESH_ID,
         ).wait_recv()
 
-    half = zs_n // 2
     last = zs_n
 
     def steps_right(k):
-        is_b = (lax.rem(k, 2) == 0) & (k > 0)
-        dist = jnp.where(lax.rem(k, 2) == 1, (k + 1) // 2, jnp.maximum(k - 2, 0) // 2)
-        x = jnp.where(is_b, 1 - me_x, me_x)
-        return x, lax.rem(me_z - dist + zs_n, zs_n)
+        x = jnp.where(lax.rem(k, 2) == 1, 1 - me_x, me_x)
+        return x, lax.rem(me_z - k // 2 + zs_n, zs_n)
 
     def steps_left(k):
-        is_b = ((lax.rem(k, 2) == 0) & (k > 0)) | (k == last - 1)
-        dist = jnp.where(lax.rem(k, 2) == 1, (k + 1) // 2, jnp.maximum(k - 2, 0) // 2)
-        dist = jnp.where(k >= last - 1, k - (last - half), dist)
-        x = jnp.where(is_b, 1 - me_x, me_x)
-        return x, lax.rem(me_z + dist, zs_n)
+        x = jnp.where((lax.rem(k, 2) == 1) | (k == last), 1 - me_x, me_x)
+        return x, lax.rem(me_z + k // 2, zs_n)
 
     def goes_right(k):
         return k <= last - 2
 
     def goes_left(k):
-        return (k != last - 3) & (k != last)
-
-    def is_own(k):
-        return (k == 0) | (k == 2)
+        return (k != last - 2) & (k != last)
+
+    own_kv.wait()
+    forward(0, right, me_x, me_z).start()
+    forward(1, left, me_x, me_z).start()
+    forward(2, sibling, me_x, me_z).start()
+
+    pages, slots = first.shape[0], table_ref.shape[1]
+    page_id = lax.broadcasted_iota(jnp.int32, (pages, slots), 0)
+    slot_id = lax.broadcasted_iota(jnp.int32, (pages, slots), 1).astype(jnp.float32)
+    offset = lax.broadcasted_iota(jnp.int32, (pages, tok), 1)
+    for r in range(2):
+        match = page_id == table_ref[r : r + 1, :]
+        slot = jnp.sum(jnp.where(match, slot_id, 0.0), axis=1, keepdims=True).astype(jnp.int32)
+        owned = jnp.sum(jnp.where(match, 1.0, 0.0), axis=1, keepdims=True)
+        visible = slot * tok + offset < length_ref[r]
+        seen[r] = jnp.where(visible, owned, 0.0)
+        if r == 0:
+            first[...] = jnp.broadcast_to(owned, (pages, tok))
+    acc[...] = jnp.zeros_like(acc)
 
     rows = 2 * tok
     lane = lax.broadcasted_iota(jnp.int32, (rows, tok), 1)
@@ -125,8 +164,8 @@
     ahead = lax.rem(row, tok) - lane
 
     def weigh(scores):
-        capped = jnp.tanh(scores * (score_scale / soft_cap)) * soft_cap
-        return jnp.exp(capped)
+        capped = jnp.tanh(scores * (score_scale / soft_cap))
+        return jnp.exp2(capped * (soft_cap * log2_e))
 
     ones = jnp.ones((3 * tok, 128), jnp.bfloat16)
 
@@ -135,94 +174,125 @@
             a, b, (((1,), (1,)), ((), ())), preferred_element_type=jnp.float32
         )
 
-    def attend(c, x, z):
+    def attend(c, x, z, which):
         key_block = (x * zs_n + z) * 2 + c
-        seen = mask_ref[key_block]
-        for r in range(2):
-            pool = pl.ds(tok, 2 * tok)
-            new = pl.ds(r * 3 * tok, tok)
-            every = pl.ds(r * tok, 3 * tok)
-            pool_k = kvbuf[c, x, z, 0, pool, :]
-            new_k = kvbuf[c, x, z, 0, new, :]
-            values = jnp.concatenate([kvbuf[c, x, z, 1, every, :], ones], axis=1)
-            for qx in range(2):
-                query = qall[qx, r]
-                query_block = (qx * zs_n + me_z) * 2 + me_c
-                w_pool = weigh(dots(query, pool_k)) * seen[r : r + 1, :]
+        for qx in which:
+            query_block = (qx * zs_n + me_z) * 2 + me_c
+            w_page = []
+            for p in range(2):
+                pick = first[pl.ds(2 * key_block + p, 1), :].astype(jnp.bfloat16)
+                query = qall[qx, 0] * pick + qall[qx, 1] * (1 - pick)
+                w_page.append(weigh(dots(query, kvbuf[c, x, z, 0, pl.ds((1 + p) * tok, tok), :])))
+            for r in range(2):
                 w_new = jnp.where(
-                    ahead >= (key_block - query_block) * tok, weigh(dots(query, new_k)), 0.0
+                    ahead >= (key_block - query_block) * tok,
+                    weigh(dots(qall[qx, r], kvbuf[c, x, z, 0, pl.ds(r * 3 * tok, tok), :])),
+                    0.0,
                 )
-                both = [w_new, w_pool] if r == 0 else [w_pool, w_new]
+                w_pool = [w_page[p] * seen[r, pl.ds(2 * key_block + p, 1), :] for p in range(2)]
+                both = [w_new] + w_pool if r == 0 else w_pool + [w_new]
                 weights = jnp.concatenate(both, axis=1).astype(jnp.bfloat16)
+                values = jnp.concatenate(
+                    [kvbuf[c, x, z, 1, pl.ds(r * tok, 3 * tok), :], ones], axis=1
+                )
                 acc[qx, r] += jnp.dot(weights, values, preferred_element_type=jnp.float32)
 
-    own_kv.wait()
-    acc[...] = jnp.zeros_like(acc)
+    own_q.wait()
+    q_swap.wait_recv()
+
+    def receive(k):
+        rx, rz = steps_right(k)
+        lx, lz = steps_left(k)
+        landed(me_c, rx, rz)
+
+        @pl.when(goes_right(k))
+        def _():
+            forward(0, right, rx, rz).start()
+
+        landed(me_c, lx, lz)
+
+        @pl.when(goes_left(k))
+        def _():
+            forward(1, left, lx, lz).start()
+
+        forward(2, sibling, rx, rz).start()
+        forward(2, sibling, lx, lz).start()
 
     def one_step(k, carry):
         rx, rz = steps_right(k)
         lx, lz = steps_left(k)
-        own = is_own(k)
-
-        @pl.when(k > 0)
-        def _():
-            landed(me_c, rx, rz)
-
-        @pl.when(goes_right(k))
-        def _():
-            forward(0, right, rx, rz).start()
-
-        @pl.when(jnp.logical_not(own))
-        def _():
-            landed(me_c, lx, lz)
-
-        @pl.when(goes_left(k))
-        def _():
-            forward(1, left, lx, lz).start()
-
-        forward(2, sibling, rx, rz).start()
-
-        @pl.when(jnp.logical_not(own))
-        def _():
-            forward(2, sibling, lx, lz).start()
-
-        @pl.when(k == 0)
-        def _():
-            own_q.wait()
-            q_swap.wait_recv()
+        own = k <= 1
+
+        @pl.when(k == 1)
+        def _():
+            for h in range(2):
+                kv_swap_landed(h)
+                forward_half(0, right, rx, rz, h).start()
+                forward_half(1, left, rx, rz, h).start()
+            forward(2, sibling, rx, rz).start()
+
+        @pl.when(k > 1)
+        def _():
+            receive(k)
 
         def one_shard(i, carry):
-            c = jnp.where(i % 2 == 0, me_c, 1 - me_c)
-            x = jnp.where(i < 2, rx, lx)
-            z = jnp.where(i < 2, rz, lz)
-
-            @pl.when(i % 2 == 1)
+            mine = jnp.where(own, 1, 2) > i
+            c = jnp.where(mine, me_c, 1 - me_c)
+            from_left = own | (lax.rem(i, 2) == 0)
+            x = jnp.where(from_left, rx, lx)
+            z = jnp.where(from_left, rz, lz)
+
+            @pl.when(jnp.logical_not(mine))
             def _():
                 landed(c, x, z)
 
-            attend(c, x, z)
+            attend(c, x, z, (0, 1))
             return carry
 
         lax.fori_loop(0, jnp.where(own, 2, 4), one_shard, 0)
         return carry
 
-    lax.fori_loop(0, last + 1, one_step, 0)
+    lax.fori_loop(0, last, one_step, 0)
 
     def finished(qx, r):
         total = acc[qx, r]
         return (total[:, :128] / total[:, 128:]).astype(jnp.bfloat16)
 
-    for r in range(2):
-        att_send[r] = finished(1 - me_x, r)
     att_swap = pltpu.make_async_remote_copy(
         src_ref=att_send,
         dst_ref=att_recv,
-        send_sem=x_send.at[2],
+        send_sem=x_send.at[1],
         recv_sem=x_recv.at[1],
         device_id=partner,
         device_id_type=MESH_ID,
     )
-    att_swap.start()
+
+    receive(last)
+    end_rx, end_rz = steps_right(last)
+    end_lx, end_lz = steps_left(last)
+
+    def end_shard(i, carry):
+        mine = lax.rem(i, 4) < 2
+        c = jnp.where(mine, me_c, 1 - me_c)
+        from_left = lax.rem(i, 2) == 0
+        x = jnp.where(from_left, end_rx, end_lx)
+        z = jnp.where(from_left, end_rz, end_lz)
+
+        @pl.when((i == 2) | (i == 3))
+        def _():
+            landed(c, x, z)
+
+        attend(c, x, z, (jnp.where(i < 4, 1 - me_x, me_x),))
+
+        @pl.when(i == 3)
+        def _():
+            for r in range(2):
+                att_send[r] = finished(1 - me_x, r)
+            att_swap.start()
+
+        return carry
+
+    lax.fori_loop(0, 8, end_shard, 0)
 
     share = tok // 8
 
@@ -238,7 +308,8 @@
         put(1 - me_x, r, att_recv[r])
 
     q_swap.wait_send()
-    kv_swap.wait_send()
+    kv_swap(0).wait_send()
+    kv_swap(1).wait_send()
 
     def drain(k, carry):
         rx, rz = steps_right(k)
@@ -254,7 +325,7 @@
 
         forward(2, sibling, rx, rz).wait_send()
 
-        @pl.when(jnp.logical_not(is_own(k)))
+        @pl.when(k > 1)
         def _():
             forward(2, sibling, lx, lz).wait_send()
 
@@ -278,14 +349,6 @@
     q = q.transpose(2, 0, 3, 1, 4).reshape(kv_heads, req, 2 * tok, dim)
 
     pages = 2 * lax.axis_size("blk")
-    slots = page_table.shape[1]
-    match = jnp.arange(pages, dtype=jnp.int32)[:, None, None] == page_table[None]
-    slot = jnp.sum(jnp.where(match, jnp.arange(slots, dtype=jnp.int32), 0), axis=2)
-    owned = jnp.any(match, axis=2)
-    position = slot[:, :, None] * tok + jnp.arange(tok, dtype=jnp.int32)
-    seen = (owned[:, :, None] & (position < cache_len[None, :, None])).astype(jnp.float32)
-    seen = seen.reshape(pages // 2, 2, req, tok).transpose(0, 2, 1, 3)
-    seen = seen.reshape(pages // 2, req, 2 * tok)
 
     hbm = pl.BlockSpec(memory_space=pl.ANY)
     vmem = pl.BlockSpec(memory_space=pltpu.VMEM)
@@ -293,22 +356,24 @@
         functools.partial(attend_kernel, zs_n, tok),
         name="gather_and_attend",
         out_shape=jax.ShapeDtypeStruct((8, req, tok // 8, heads * dim), jnp.bfloat16),
-        in_specs=[hbm, hbm, vmem],
+        in_specs=[hbm, hbm, vmem, pl.BlockSpec(memory_space=pltpu.SMEM)],
         out_specs=vmem,
         scratch_shapes=[
             pltpu.VMEM((2, 2, zs_n, 2, 4 * tok, dim), jnp.bfloat16),
             pltpu.VMEM((2, req, 2 * tok, dim), jnp.bfloat16),
             pltpu.VMEM((2, req, 2 * tok, 2 * dim), jnp.float32),
+            pltpu.VMEM((req, pages, tok), jnp.float32),
+            pltpu.VMEM((pages, tok), jnp.float32),
             pltpu.VMEM((req, 2 * tok, dim), jnp.bfloat16),
             pltpu.VMEM((req, 2 * tok, dim), jnp.bfloat16),
             pltpu.SemaphoreType.DMA((2,)),
             pltpu.SemaphoreType.DMA((3, 2, zs_n)),
             pltpu.SemaphoreType.DMA((2, 2, zs_n)),
-            pltpu.SemaphoreType.DMA((3,)),
-            pltpu.SemaphoreType.DMA((2,)),
+            pltpu.SemaphoreType.DMA((4,)),
+            pltpu.SemaphoreType.DMA((4,)),
         ],
         compiler_params=pltpu.CompilerParams(collective_id=0, has_side_effects=True),
-    )(kv, q, seen)
+    )(kv, q, page_table, cache_len)
 
 
 def project_kernel(

time: 113 us -> 106 us (0.938)
  Pallas kernels: 99.9 us -> 96 us
  other arithmetic: 3.8 us -> 0.87 us
    pallas_call x1, Pallas kernels: 63.3 us -> 59.2 us  [gather_and_attend(): pl.pallas_call(functools.partial(attend_kernel, zs_n, tok), name='gather_...]
    convert_element_type x1 -> x0, other arithmetic: 1.38 us -> none  [gather_and_attend(): (owned[:, :, None] & (position < cache_len[None, :, None])).astype(jnp.fl...]
where the time goes in v3:
time: 106 us; the launch traced here: 105 us
  Pallas kernels  96 us (91%)
  local copies, waits for them, and re-layouts  7.73 us (7%)
    pallas_call x1, Pallas kernels, gather_and_attend(): pl.pallas_call(functools.partial(attend_kernel, zs_n, tok), name='gather_...  59.2 us
    pallas_call x1, Pallas kernels, project_and_mix(): pl.pallas_call(project_kernel, name='project_and_mix', out_shape=jax.Shap...  36.8 us
    unnamed x5, local copies, waits for them, and re-layouts  3.55 us

profile of v3, /device:TPU:32, one launch (start us, length us, event | category | flops | bytes accessed | tf_op | source)
XLA Modules:
  0.0 104.6 jit_solution(15857401283199829888)
XLA Ops:
  0.0 0.0 copy-start
  0.0 0.9 copy.19
  1.0 0.9 copy.18
  1.9 0.9 copy.12
  2.8 0.9 copy.14
  3.8 0.8 pad_maximum_fusion.kv_hbm
  4.6 1.7 %copy.15 = bf16[2,128,2,2,128]{4,1,3,0,2:T(8,128)(2,1)} copy(bf16[2,128,2,2,128]{4,3,2,1,0:T(2,128)(2,1)} %bitcast.33) | data formatting | bytes 524288 | tf_op jit(solution)/shard_map/reshape | solution.py:348
  6.3 59.2 %gather_and_attend.1.att_ref = bf16[8,2,16,512]{3,2,1,0:T(8,128)(2,1)} custom-call(bf16[2,2,512,128]{3,2,1,0:T(8,128)(2,1)} %pad_maximum_fusion.kv_hbm, bf16[2,2,256,128]{3,2,1,0:T(8,128)(2,1)} %bitcast.28, s32[2,32]{1,0:T(2,128)} %table_ref.1, s32[2]{0:T(128)} %length_ref.1), custom_call_target="tpu_custom_call" | custom-call | tf_op jit(solution)/shard_map/gather_and_attend/pallas_call | solution.py:355
  65.5 0.0 copy-done
  65.6 0.6 reshape.23.gain_ref
  66.2 36.8 %project_and_mix.1 = bf16[2,16,4608]{2,1,0:T(8,128)(2,1)} custom-call(bf16[8,2,16,512]{3,2,1,0:T(8,128)(2,1)} %gather_and_attend.1.att_ref, bf16[512,4608]{1,0:T(8,128)(2,1)} %bitcast.27, bf16[2,16,4608]{2,1,0:T(8,128)(2,1)} %residual_ref.1, f32[1,4608]{1,0:T(1,128)} %reshape.23.gain_ref), custom_call_target="tpu_custom_call" | custom-call | tf_op jit(solution)/shard_map/project_and_mix/pallas_call | solution.py:469
  102.9 1.7 %copy.21 = bf16[2,16,4608]{2,1,0:T(8,128)(2,1)} copy(bf16[2,16,4608]{2,1,0:T(8,128)(2,1)} %project_and_mix.1) | data formatting | bytes 589824
  (3 shorter events, 0.1 us)
Async XLA Ops:
  0.0 65.5 %copy-start = (f32[4608]{0:T(1024)S(1)}, f32[4608]{0:T(1024)}, u32[]{:S(2)}) copy-start(f32[4608]{0:T(1024)} %param.19) | copy-start | bytes 55300

commit v4 on v3

--- a/solution.py
+++ b/solution.py
@@ -113,6 +113,19 @@
             device_id_type=MESH_ID,
         )
 
+    def first_sends():
+        for way, device in ((0, right), (1, left), (2, sibling)):
+            pltpu.make_async_remote_copy(
+                src_ref=kv_hbm.at[me_x],
+                dst_ref=kvbuf.at[me_c, me_x, me_z],
+                send_sem=send_sem.at[way, me_x, me_z],
+                recv_sem=recv_sem.at[me_c, me_x, me_z],
+                device_id=device,
+                device_id_type=MESH_ID,
+            ).start()
+
+    first_sends()
+
     def landed(c, x, z):
         pltpu.make_async_remote_copy(
             src_ref=kvbuf.at[c, x, z],
@@ -139,10 +152,6 @@
     def goes_left(k):
         return (k != last - 2) & (k != last)
 
-    own_kv.wait()
-    forward(0, right, me_x, me_z).start()
-    forward(1, left, me_x, me_z).start()
-    forward(2, sibling, me_x, me_z).start()
 
     pages, slots = first.shape[0], table_ref.shape[1]
     page_id = lax.broadcasted_iota(jnp.int32, (pages, slots), 0)
@@ -197,6 +206,7 @@
                 )
                 acc[qx, r] += jnp.dot(weights, values, preferred_element_type=jnp.float32)
 
+    own_kv.wait()
     own_q.wait()
     q_swap.wait_recv()
 
@@ -334,20 +344,49 @@
     lax.fori_loop(0, last + 1, drain, 0)
 
 
+def lay_out_kernel(q_ref, nk_ref, nv_ref, pk_ref, pv_ref, kv_ref, q_out):
+    def by_head(ref, i, heads):
+        rows = ref.shape[1]
+        tok = rows // heads
+        row = lax.broadcasted_iota(jnp.int32, (rows, rows), 0)
+        column = lax.broadcasted_iota(jnp.int32, (rows, rows), 1)
+        source = lax.rem(row, tok) * heads + row // tok
+        order = jnp.where(source == column, 1.0, 0.0).astype(jnp.bfloat16)
+        moved = jnp.dot(order, ref[i], preferred_element_type=jnp.float32)
+        return moved.astype(jnp.bfloat16)
+
+    tok = nk_ref.shape[1] // 2
+    for n, (new, pool) in enumerate(((nk_ref, pk_ref), (nv_ref, pv_ref))):
+        for ref, i, at in ((new, 0, 0), (pool, 0, 1), (pool, 1, 2), (new, 1, 3)):
+            moved = by_head(ref, i, 2)
+            for k in range(2):
+                kv_ref[k, n, at * tok : (at + 1) * tok] = moved[k * tok : (k + 1) * tok]
+    for r in range(2):
+        moved = by_head(q_ref, r, 4)
+        for k in range(2):
+            q_out[k, r] = moved[2 * k * tok : 2 * (k + 1) * tok]
+
+
+def lay_out(queries, new_keys, new_values, pool_keys, pool_values):
+    req, tok, heads, dim = queries.shape
+    rows = [a.reshape(2, -1, dim) for a in (queries, new_keys, new_values, pool_keys, pool_values)]
+    vmem = pl.BlockSpec(memory_space=pltpu.VMEM)
+    return pl.pallas_call(
+        lay_out_kernel,
+        name="lay_out",
+        out_shape=(
+            jax.ShapeDtypeStruct((2, 2, 4 * tok, dim), jnp.bfloat16),
+            jax.ShapeDtypeStruct((2, req, 2 * tok, dim), jnp.bfloat16),
+        ),
+        in_specs=[vmem] * 5,
+        out_specs=(vmem, vmem),
+    )(*rows)
+
+
 def gather_and_attend(queries, new_keys, new_values, pool_keys, pool_values, page_table, cache_len):
     req, tok, heads, dim = queries.shape
-    kv_heads = new_keys.shape[2]
     zs_n = lax.axis_size("blk") // 4
-
-    def laid(new, pool):
-        new = new.transpose(2, 0, 1, 3)
-        pool = pool.transpose(2, 0, 1, 3).reshape(kv_heads, 2 * tok, dim)
-        return jnp.concatenate([new[:, 0], pool, new[:, 1]], axis=1)
-
-    kv = jnp.stack([laid(new_keys, pool_keys), laid(new_values, pool_values)], axis=1)
-    q = queries.reshape(req, tok, kv_heads, heads // kv_heads, dim)
-    q = q.transpose(2, 0, 3, 1, 4).reshape(kv_heads, req, 2 * tok, dim)
-
+    kv, q = lay_out(queries, new_keys, new_values, pool_keys, pool_values)
     pages = 2 * lax.axis_size("blk")
 
     hbm = pl.BlockSpec(memory_space=pl.ANY)
@@ -381,16 +420,22 @@
 ):
     me = lax.axis_index("head")
     me_y, me_h = me // 2, lax.rem(me, 2)
-    thirds = 3
-    wide = part.shape[2] // thirds
     tile = 512
+    chunks = part.shape[2] // tile
+
+    def chunk(t):
+        return pl.ds(pl.multiple_of(t * tile, tile), tile)
 
     def loads(t):
-        columns = pl.ds(t * wide, wide)
-        return pltpu.make_async_copy(weight_hbm.at[:, columns], weight.at[:, columns], w_sem.at[t])
-
-    for t in range(thirds):
+        return pltpu.make_async_copy(
+            weight_hbm.at[:, chunk(t)], weight.at[:, chunk(t)], w_sem.at[t]
+        )
+
+    def load(t, carry):
         loads(t).start()
+        return carry
+
+    lax.fori_loop(0, chunks, load, 0)
 
     peers = []
     for dy, dh in ((1, 0), (3, 0), (0, 1), (2, 0), (1, 1), (3, 1), (2, 1)):
@@ -403,11 +448,10 @@
         pl.semaphore_signal(barrier, inc=1, device_id={"head": to}, device_id_type=MESH_ID)
 
     def sends(i, t):
-        columns = pl.ds(t * wide, wide)
         to = peers[i][0]
         return pltpu.make_async_remote_copy(
-            src_ref=part.at[to, :, columns],
-            dst_ref=got.at[i, :, columns],
+            src_ref=part.at[to, :, chunk(t)],
+            dst_ref=got.at[i, :, chunk(t)],
             send_sem=send_sem.at[t, i],
             recv_sem=recv_sem.at[t, i],
             device_id={"head": to},
@@ -415,36 +459,28 @@
         )
 
     attended = att_ref[...].reshape(8 * 32, att_ref.shape[3])
-    for t in range(thirds):
+    pl.semaphore_wait(barrier, 7)
+
+    def one_chunk(t, carry):
         loads(t).wait()
-
-        def one_tile(i, carry):
-            columns = pl.ds(pl.multiple_of(t * wide + i * tile, tile), tile)
-            value = jnp.dot(attended, weight[:, columns], preferred_element_type=jnp.float32)
-            part[:, :, columns] = value.astype(jnp.bfloat16).reshape(8, 32, tile)
-            return carry
-
-        lax.fori_loop(0, wide // tile, one_tile, 0)
-        if t == 0:
-            pl.semaphore_wait(barrier, 7)
+        value = jnp.dot(attended, weight[:, chunk(t)], preferred_element_type=jnp.float32)
+        part[:, :, chunk(t)] = value.astype(jnp.bfloat16).reshape(8, 32, tile)
         for i in range(7):
             sends(i, t).start()
-
-    square = jnp.zeros((32, 1), jnp.float32)
-    for t in range(thirds):
+        return carry
+
+    lax.fori_loop(0, chunks, one_chunk, 0)
+
+    def add_chunk(t, square):
         for i in range(7):
             sends(i, t).wait_recv()
-
-        def add_tile(n, square):
-            columns = pl.ds(pl.multiple_of(t * wide + n * tile, tile), tile)
-            value = part[me, :, columns].astype(jnp.float32)
-            for i in range(7):
-                value = value + got[i, :, columns].astype(jnp.float32)
-            total[:, columns] = value
-            return square + jnp.sum(value * value, axis=1, keepdims=True)
-
-        square = lax.fori_loop(0, wide // tile, add_tile, square)
-
+        value = part[me, :, chunk(t)].astype(jnp.float32)
+        for i in range(7):
+            value = value + got[i, :, chunk(t)].astype(jnp.float32)
+        total[:, chunk(t)] = value
+        return square + jnp.sum(value * value, axis=1, keepdims=True)
+
+    square = lax.fori_loop(0, chunks, add_chunk, jnp.zeros((32, 1), jnp.float32))
     inv_rms = lax.rsqrt(square / part.shape[2] + norm_eps)
 
     def mix_tile(n, carry):
@@ -457,10 +493,14 @@
             )
         return carry
 
-    lax.fori_loop(0, part.shape[2] // tile, mix_tile, 0)
-    for t in range(thirds):
+    lax.fori_loop(0, chunks, mix_tile, 0)
+
+    def drain(t, carry):
         for i in range(7):
             sends(i, t).wait_send()
+        return carry
+
+    lax.fori_loop(0, chunks, drain, 0)
 
 
 def project_and_mix(attended, weight_rows, residual, post_gain):
@@ -477,9 +517,9 @@
             pltpu.VMEM((8, 32, width), jnp.bfloat16),
             pltpu.VMEM((7, 32, width), jnp.bfloat16),
             pltpu.VMEM((32, width), jnp.float32),
-            pltpu.SemaphoreType.DMA((3,)),
-            pltpu.SemaphoreType.DMA((3, 7)),
-            pltpu.SemaphoreType.DMA((3, 7)),
+            pltpu.SemaphoreType.DMA((width // 512,)),
+            pltpu.SemaphoreType.DMA((width // 512, 7)),
+            pltpu.SemaphoreType.DMA((width // 512, 7)),
         ],
         compiler_params=pltpu.CompilerParams(collective_id=1, has_side_effects=True),
     )(attended, weight_rows, residual, post_gain.reshape(1, width))

time: 106 us -> 102 us (0.962)
  local copies, waits for them, and re-layouts: 7.73 us -> 3.04 us
  Pallas kernels: 96 us -> 98.2 us
    pallas_call x0 -> x1, Pallas kernels: none -> 2.55 us  [lay_out(): pl.pallas_call(lay_out_kernel, name='lay_out', out_shape=(jax.ShapeDtypeS...]
    unnamed x5 -> x1, local copies, waits for them, and re-layouts: 3.55 us -> 1.69 us
    transpose x2 -> x0, local copies, waits for them, and re-layouts: 1.85 us -> none  [laid(): pool = pool.transpose(2, 0, 1, 3).reshape(kv_heads, 2 * tok, dim)]
    reshape x1 -> x0, local copies, waits for them, and re-layouts: 1.69 us -> none  [gather_and_attend(): q = queries.reshape(req, tok, kv_heads, heads // kv_heads, dim)]
where the time goes in v4:
time: 102 us; the launch traced here: 101 us
  Pallas kernels  98.2 us (96%)
  local copies, waits for them, and re-layouts  3.04 us (3%)
    pallas_call x1, Pallas kernels, gather_and_attend(): pl.pallas_call(functools.partial(attend_kernel, zs_n, tok), name='gather_...  59.2 us
    pallas_call x1, Pallas kernels, project_and_mix(): pl.pallas_call(project_kernel, name='project_and_mix', out_shape=jax.Shap...  36.4 us
    pallas_call x1, Pallas kernels, lay_out(): pl.pallas_call(lay_out_kernel, name='lay_out', out_shape=(jax.ShapeDtypeS...  2.55 us

profile of v4, /device:TPU:32, one launch (start us, length us, event | category | flops | bytes accessed | tf_op | source)
XLA Modules:
  0.0 101.2 jit_solution(6413045159972929036)
XLA Ops:
  0.0 2.6 %lay_out.1 = (bf16[2,2,512,128]{3,2,1,0:T(8,128)(2,1)}, bf16[2,2,256,128]{3,2,1,0:T(8,128)(2,1)}) custom-call(bf16[2,512,128]{2,1,0:T(8,128)(2,1)} %bitcast.7, bf16[2,256,128]{2,1,0:T(8,128)(2,1)} %bitcast.8, bf16[2,256,128]{2,1,0:T(8,128)(2,1)} %bitcast.9, bf16[2,256,128]{2,1,0:T(8,128)(2,1)} %bitcast.10, bf16[2,256,128]{2,1,0:T(8,128)(2,1)} %bitcast.11), custom_call_target="tpu_custom_call" | custom-call | tf_op jit(solution)/shard_map/lay_out/pallas_call | solution.py:374
  2.6 59.2 %gather_and_attend.1.att_ref = bf16[8,2,16,512]{3,2,1,0:T(8,128)(2,1)} custom-call(bf16[2,2,512,128]{3,2,1,0:T(8,128)(2,1)} %get-tuple-element.7.kv_hbm, bf16[2,2,256,128]{3,2,1,0:T(8,128)(2,1)} %get-tuple-element.8.q_hbm, s32[2,32]{1,0:T(2,128)} %table_ref.1, s32[2]{0:T(128)} %length_ref.1), custom_call_target="tpu_custom_call" | custom-call | tf_op jit(solution)/shard_map/gather_and_attend/pallas_call | solution.py:394
  61.8 1.3 %reshape.27.gain_ref = f32[1,4608]{1,0:T(1,128)} reshape(f32[4608]{0:T(1024)} %param.19) | data formatting | bytes 36864 | tf_op jit(solution)/shard_map/reshape | solution.py:525
  63.1 36.4 %project_and_mix.1 = bf16[2,16,4608]{2,1,0:T(8,128)(2,1)} custom-call(bf16[8,2,16,512]{3,2,1,0:T(8,128)(2,1)} %gather_and_attend.1.att_ref, bf16[512,4608]{1,0:T(8,128)(2,1)} %bitcast.6, bf16[2,16,4608]{2,1,0:T(8,128)(2,1)} %residual_ref.1, f32[1,4608]{1,0:T(1,128)} %reshape.27.gain_ref), custom_call_target="tpu_custom_call" | custom-call | tf_op jit(solution)/shard_map/project_and_mix/pallas_call | solution.py:509
  99.5 1.7 %copy.12 = bf16[2,16,4608]{2,1,0:T(8,128)(2,1)} copy(bf16[2,16,4608]{2,1,0:T(8,128)(2,1)} %project_and_mix.1) | data formatting | bytes 589824

commit v5 on v4

--- a/solution.py
+++ b/solution.py
@@ -89,9 +89,9 @@
             device_id_type=MESH_ID,
         ).wait_recv()
 
-    q_swap.start()
     kv_swap(0).start()
     kv_swap(1).start()
+    q_swap.start()
 
     def forward(way, device, x, z):
         return pltpu.make_async_remote_copy(
@@ -207,6 +207,11 @@
                 acc[qx, r] += jnp.dot(weights, values, preferred_element_type=jnp.float32)
 
     own_kv.wait()
+    for h in range(2):
+        kv_swap_landed(h)
+        forward_half(0, right, 1 - me_x, me_z, h).start()
+        forward_half(1, left, 1 - me_x, me_z, h).start()
+    forward(2, sibling, 1 - me_x, me_z).start()
     own_q.wait()
     q_swap.wait_recv()
 
@@ -232,14 +237,6 @@
         rx, rz = steps_right(k)
         lx, lz = steps_left(k)
         own = k <= 1
-
-        @pl.when(k == 1)
-        def _():
-            for h in range(2):
-                kv_swap_landed(h)
-                forward_half(0, right, rx, rz, h).start()
-                forward_half(1, left, rx, rz, h).start()
-            forward(2, sibling, rx, rz).start()
 
         @pl.when(k > 1)
         def _():
@@ -485,7 +482,8 @@
 
     def mix_tile(n, carry):
         columns = pl.ds(pl.multiple_of(n * tile, tile), tile)
-        value = gain_ref[:, columns] * total[:, columns] * inv_rms
+        gain = [gain_ref[pl.ds(n * (tile // 128) + j, 1), :] for j in range(tile // 128)]
+        value = jnp.concatenate(gain, axis=1) * total[:, columns] * inv_rms
         for r in range(2):
             rows = value[r * 16 : (r + 1) * 16]
             out_ref[r, :, columns] = (residual_ref[r, :, columns].astype(jnp.float32) + rows).astype(
@@ -522,7 +520,7 @@
             pltpu.SemaphoreType.DMA((width // 512, 7)),
         ],
         compiler_params=pltpu.CompilerParams(collective_id=1, has_side_effects=True),
-    )(attended, weight_rows, residual, post_gain.reshape(1, width))
+    )(attended, weight_rows, residual, post_gain.reshape(width // 128, 128))
 
 
 def shards(

time: 102 us -> 99.9 us (0.979)
  local copies, waits for them, and re-layouts: 3.04 us -> 1.69 us
  Pallas kernels: 98.2 us -> 96.9 us
    pallas_call x1, Pallas kernels: 59.2 us -> 57.8 us  [gather_and_attend(): pl.pallas_call(functools.partial(attend_kernel, zs_n, tok), name='gather_...]
    reshape x1 -> x0, local copies, waits for them, and re-layouts: 1.35 us -> none  [project_and_mix(): post_gain.reshape(1, width)]
where the time goes in v5:
time: 99.9 us; the launch traced here: 98.6 us
  Pallas kernels  96.9 us (97%)
  local copies, waits for them, and re-layouts  1.69 us (2%)
    pallas_call x1, Pallas kernels, gather_and_attend(): pl.pallas_call(functools.partial(attend_kernel, zs_n, tok), name='gather_...  57.8 us
    pallas_call x1, Pallas kernels, project_and_mix(): pl.pallas_call(project_kernel, name='project_and_mix', out_shape=jax.Shap...  36.5 us
    pallas_call x1, Pallas kernels, lay_out(): pl.pallas_call(lay_out_kernel, name='lay_out', out_shape=(jax.ShapeDtypeS...  2.55 us

profile of v5, /device:TPU:32, one launch (start us, length us, event | category | flops | bytes accessed | tf_op | source)
XLA Modules:
  0.0 98.6 jit_solution(3284394789257907856)
XLA Ops:
  0.0 2.6 %lay_out.1 = (bf16[2,2,512,128]{3,2,1,0:T(8,128)(2,1)}, bf16[2,2,256,128]{3,2,1,0:T(8,128)(2,1)}) custom-call(bf16[2,512,128]{2,1,0:T(8,128)(2,1)} %bitcast.8, bf16[2,256,128]{2,1,0:T(8,128)(2,1)} %bitcast.9, bf16[2,256,128]{2,1,0:T(8,128)(2,1)} %bitcast.10, bf16[2,256,128]{2,1,0:T(8,128)(2,1)} %bitcast.11, bf16[2,256,128]{2,1,0:T(8,128)(2,1)} %bitcast.12), custom_call_target="tpu_custom_call" | custom-call | tf_op jit(solution)/shard_map/lay_out/pallas_call | solution.py:371
  2.6 57.8 %gather_and_attend.1.att_ref = bf16[8,2,16,512]{3,2,1,0:T(8,128)(2,1)} custom-call(bf16[2,2,512,128]{3,2,1,0:T(8,128)(2,1)} %get-tuple-element.7.kv_hbm, bf16[2,2,256,128]{3,2,1,0:T(8,128)(2,1)} %get-tuple-element.8.q_hbm, s32[2,32]{1,0:T(2,128)} %table_ref.1, s32[2]{0:T(128)} %length_ref.1), custom_call_target="tpu_custom_call" | custom-call | tf_op jit(solution)/shard_map/gather_and_attend/pallas_call | solution.py:391
  60.4 36.5 %project_and_mix.1 = bf16[2,16,4608]{2,1,0:T(8,128)(2,1)} custom-call(bf16[8,2,16,512]{3,2,1,0:T(8,128)(2,1)} %gather_and_attend.1.att_ref, bf16[512,4608]{1,0:T(8,128)(2,1)} %bitcast.7, bf16[2,16,4608]{2,1,0:T(8,128)(2,1)} %residual_ref.1, f32[36,128]{1,0:T(8,128)} %bitcast.13), custom_call_target="tpu_custom_call" | custom-call | tf_op jit(solution)/shard_map/project_and_mix/pallas_call | solution.py:507
  96.9 1.7 %copy.12 = bf16[2,16,4608]{2,1,0:T(8,128)(2,1)} copy(bf16[2,16,4608]{2,1,0:T(8,128)(2,1)} %project_and_mix.1) | data formatting | bytes 589824
